TPU v7x, 32 devices: a whole 2x2x4 slice. The times are simulated.
32 devices in a mesh: req: 4 (over z), exp: 8 (over y, x, core).
Axes of the slice: x: 2, y: 2, z: 4, core: 2. Of those that a mesh axis runs over, the one named last changes fastest.
Arguments:
- queries: bfloat16 [64, 32, 2304], P(('req', 'exp')), may hold values from -8 to 8
- draft_keys: bfloat16 [64, 32, 2304], P(('req', 'exp')), may hold values from -9 to 9
- draft_values: bfloat16 [64, 32, 2304], P(('req', 'exp')), may hold values from -6 to 6
- tree_parents: int32 [64, 32], P(('req', 'exp')), may hold values from -1 to 30, as said below
- cache_keys: bfloat16 [64, 768, 2304], P(('req', 'exp')), may hold values from -9 to 9
- cache_values: bfloat16 [64, 768, 2304], P(('req', 'exp')), may hold values from -6 to 6
- cache_lengths: int32 [64], P(('req', 'exp')), may hold values from 1 to 768, as said below
- prompt_keys: bfloat16 [8, 512, 2304], P('req', 'exp'), may hold values from -9 to 9
- prompt_values: bfloat16 [8, 512, 2304], P('req', 'exp'), may hold values from -6 to 6
- group_ids: int32 [64], P(('req', 'exp')), may hold values from 0 to 1
- residual: bfloat16 [64, 32, 2304], P(('req', 'exp')), may hold values from -6 to 6
- norm_gain: float32 [2304], replicated, may hold values from 0.5 to 1.5
- router: bfloat16 [2304, 8], replicated, may hold values from -0.125 to 0.125
- w_gate: bfloat16 [8, 2304, 5760], P('exp', None, 'req'), may hold values from -0.125 to 0.125
- w_up: bfloat16 [8, 2304, 5760], P('exp', None, 'req'), may hold values from -0.125 to 0.125
- w_down: bfloat16 [8, 5760, 2304], P('exp', 'req'), may hold values from -0.078125 to 0.078125
- expert_ids: int32 [64, 32, 2], P(('req', 'exp')), may hold values from 0 to 7, all different within a row; in each aligned block of 64 rows (0 to 63, 64 to 127, ..., all dimensions but the last counted through in order) at most 18 rows name the same one
- accepted_rows: int32 [64, 8], P(('req', 'exp')), may hold values from 0 to 31
Outputs:
- attended: bfloat16 [64, 32, 2304], P(('req', 'exp'))
- layer_out: bfloat16 [64, 32, 2304], P(('req', 'exp'))
- accepted_cache: bfloat16 [64, 2, 8, 2304], P(('req', 'exp'))
Inputs may be any that keep to these rules, and one draw needn't show every extreme that they name: `tree_parents`: position 0 of every tree holds -1; every other position holds an earlier position of the same tree. `cache_lengths`: some request has all 768 slots used. `expert_ids`: the two experts of a position differ; among the rows of one device no expert is named more than 18 times, a bound that some block reaches.
All inputs are finite; a program needn't handle non-finite values.
Results may differ from a plain program's by a relative error of at most 0.013.
Values may be sent and summed in bfloat16 or wider, within the bound.
A program may use at most 192 MiB of HBM per device.

v0:
```python
import jax
import jax.numpy as jnp
from jax import lax
from jax.sharding import PartitionSpec as P

HEADS = 36
HDIM = 64
EXPERTS = 8
TOPK = 2
GRP = 2
CAP = 18
HIGH = lax.Precision.HIGHEST
EPSILON = 1e-05


def ancestry(parents):
    length = parents.shape[-1]
    column = jnp.arange(length, dtype=jnp.int32)
    reached = (parents[..., :, None] == column).astype(jnp.float32) + jnp.eye(
        length, dtype=jnp.float32
    )
    for repeat in range(max(1, (length - 1).bit_length())):
        reached = (jnp.einsum("...ij,...jk->...ik", reached, reached, precision=HIGH) > 0.5).astype(
            jnp.float32
        )
    return reached > 0.5


def slot_numbers(picked_ids):
    flattened = picked_ids.reshape(-1)
    onehot = (flattened[:, None] == jnp.arange(EXPERTS, dtype=jnp.int32)[None, :]).astype(jnp.int32)
    before = jnp.cumsum(onehot, axis=0) - onehot
    return jnp.sum(before * onehot, axis=1).reshape(picked_ids.shape)


def on_device(
    queries,
    draft_keys,
    draft_values,
    tree_parents,
    cache_keys,
    cache_values,
    cache_lengths,
    prompt_keys,
    prompt_values,
    group_ids,
    residual,
    norm_gain,
    router,
    w_gate,
    w_up,
    w_down,
    expert_ids,
    accepted_rows,
):
    requests, tree_len, width = queries.shape
    row_count = requests * tree_len
    score_scale = HDIM ** (-0.5)
    heads_q = queries.reshape(requests, tree_len, HEADS, HDIM)
    cache_heads = cache_keys.reshape(requests, -1, HEADS, HDIM)
    cache_vals = cache_values.reshape(requests, -1, HEADS, HDIM)
    cache_scores = (
        jnp.einsum("bthd,bchd->bthc", heads_q, cache_heads, preferred_element_type=jnp.float32)
        * score_scale
    )
    live_cache = jnp.arange(cache_heads.shape[1], dtype=jnp.int32)[None, :] < cache_lengths[:, None]
    cache_scores = jnp.where(live_cache[:, None, None, :], cache_scores, -jnp.inf)
    draft_heads = draft_keys.reshape(requests, tree_len, HEADS, HDIM)
    draft_vals = draft_values.reshape(requests, tree_len, HEADS, HDIM)
    tree_scores = (
        jnp.einsum("bthd,bshd->bths", heads_q, draft_heads, preferred_element_type=jnp.float32)
        * score_scale
    )
    tree_scores = jnp.where(ancestry(tree_parents)[:, :, None, :], tree_scores, -jnp.inf)
    local_top = jnp.maximum(jnp.max(cache_scores, axis=-1), jnp.max(tree_scores, axis=-1))
    cache_weights = jnp.exp(cache_scores - local_top[..., None])
    tree_weights = jnp.exp(tree_scores - local_top[..., None])
    local_total = jnp.sum(cache_weights, axis=-1) + jnp.sum(tree_weights, axis=-1)
    local_acc = jnp.einsum(
        "bthc,bchd->bthd",
        cache_weights.astype(jnp.bfloat16),
        cache_vals,
        preferred_element_type=jnp.float32,
    )
    local_acc = local_acc + jnp.einsum(
        "bths,bshd->bthd",
        tree_weights.astype(jnp.bfloat16),
        draft_vals,
        preferred_element_type=jnp.float32,
    )
    local_top = local_top.reshape(row_count, HEADS)
    local_total = local_total.reshape(row_count, HEADS)
    local_acc = local_acc.reshape(row_count, HEADS, HDIM)
    member = jnp.repeat(group_ids, tree_len)[:, None] == jnp.arange(GRP, dtype=jnp.int32)[None, :]
    query_rows = heads_q.reshape(row_count, HEADS, HDIM)
    running_top = local_top
    summed = local_total
    gathered_acc = local_acc
    key_piece = lax.all_gather(prompt_keys, "exp", axis=1, tiled=True)
    value_piece = lax.all_gather(prompt_values, "exp", axis=1, tiled=True)
    key_count = key_piece.shape[1]
    key_heads = key_piece.reshape(GRP, key_count, HEADS, HDIM)
    value_heads = value_piece.reshape(GRP, key_count, HEADS, HDIM)
    block_scores = (
        jnp.einsum("rhd,gkhd->rhgk", query_rows, key_heads, preferred_element_type=jnp.float32)
        * score_scale
    )
    block_scores = jnp.where(member[:, None, :, None], block_scores, -jnp.inf)
    new_top = jnp.maximum(running_top, jnp.max(block_scores, axis=(2, 3)))
    shrink = jnp.exp(running_top - new_top)
    block_weights = jnp.exp(block_scores - new_top[:, :, None, None])
    summed = summed * shrink + jnp.sum(block_weights, axis=(2, 3))
    gathered_acc = gathered_acc * shrink[:, :, None] + jnp.einsum(
        "rhgk,gkhd->rhd",
        block_weights.astype(jnp.bfloat16),
        value_heads,
        preferred_element_type=jnp.float32,
    )
    running_top, summed, gathered_acc = (new_top, summed, gathered_acc)
    attended = (
        (gathered_acc / summed[:, :, None]).reshape(requests, tree_len, width).astype(jnp.bfloat16)
    )
    stream = (residual.astype(jnp.float32) + attended.astype(jnp.float32)).astype(jnp.bfloat16)
    stream_rows = stream.reshape(row_count, width).astype(jnp.float32)
    normed = (
        stream_rows
        * lax.rsqrt(jnp.mean(stream_rows * stream_rows, axis=-1, keepdims=True) + EPSILON)
        * norm_gain
    ).astype(jnp.bfloat16)
    logits = jnp.dot(normed, router, preferred_element_type=jnp.float32)
    routed = expert_ids.reshape(row_count, TOPK)
    chosen = jnp.take_along_axis(logits, routed, axis=1)
    gate_first = 1.0 / (1.0 + jnp.exp(chosen[:, 1] - chosen[:, 0]))
    gates = jnp.stack([gate_first, 1.0 - gate_first], axis=1)
    target = routed * CAP + slot_numbers(routed)
    buffer = (
        jnp.zeros((EXPERTS * CAP, width), jnp.bfloat16)
        .at[target.reshape(-1)]
        .set(jnp.repeat(normed, TOPK, axis=0))
    )
    holder_count = lax.axis_size("exp")
    holders = holder_count // EXPERTS
    outgoing = jnp.broadcast_to(
        buffer.reshape(EXPERTS, 1, CAP, width), (EXPERTS, holders, CAP, width)
    ).reshape(holder_count, CAP, width)
    gate_local = w_gate[0]
    up_local = w_up[0]
    down_local = w_down[0]
    arrived = lax.all_to_all(outgoing, "exp", split_axis=0, concat_axis=0, tiled=True)
    row_piece = lax.all_gather(arrived.reshape(-1, width), "req", axis=0, tiled=True)
    gate_proj = jnp.dot(row_piece, gate_local, preferred_element_type=jnp.float32)
    up_proj = jnp.dot(row_piece, up_local, preferred_element_type=jnp.float32)
    hidden = (jax.nn.silu(gate_proj) * up_proj).astype(jnp.bfloat16)
    summed_rows = lax.psum_scatter(
        jnp.dot(hidden, down_local, preferred_element_type=jnp.float32).astype(jnp.bfloat16),
        "req",
        scatter_dimension=0,
        tiled=True,
    )
    returned = lax.all_to_all(
        summed_rows.reshape(holder_count, CAP, width),
        "exp",
        split_axis=0,
        concat_axis=0,
        tiled=True,
    )
    expert_result = (
        returned.astype(jnp.float32)
        .reshape(EXPERTS, holders, CAP, width)
        .sum(axis=1)
        .reshape(EXPERTS * CAP, width)
    )
    picked = expert_result[target]
    layer_out = (
        (stream_rows + jnp.sum(gates[:, :, None] * picked, axis=1))
        .astype(jnp.bfloat16)
        .reshape(requests, tree_len, width)
    )
    kept_keys = jnp.take_along_axis(draft_keys, accepted_rows[:, :, None], axis=1)
    kept_values = jnp.take_along_axis(draft_values, accepted_rows[:, :, None], axis=1)
    accepted_cache = jnp.stack([kept_keys, kept_values], axis=1)
    return (attended, layer_out, accepted_cache)


def solution(mesh):
    return jax.shard_map(
        on_device,
        mesh=mesh,
        in_specs=(
            P(("req", "exp"), None, None),
            P(("req", "exp"), None, None),
            P(("req", "exp"), None, None),
            P(("req", "exp"), None),
            P(("req", "exp"), None, None),
            P(("req", "exp"), None, None),
            P(("req", "exp")),
            P("req", "exp", None),
            P("req", "exp", None),
            P(("req", "exp")),
            P(("req", "exp"), None, None),
            P(),
            P(),
            P("exp", None, "req"),
            P("exp", None, "req"),
            P("exp", "req", None),
            P(("req", "exp"), None, None),
            P(("req", "exp"), None),
        ),
        out_specs=(
            P(("req", "exp"), None, None),
            P(("req", "exp"), None, None),
            P(("req", "exp"), None, None, None),
        ),
        check_vma=False,
    )
```

profile of v0, /device:TPU:0, one launch (start us, length us, event | category | flops | bytes accessed | tf_op | source)
XLA Modules:
  0.0 296.1 jit_solution(12981081108997633056)
XLA Ops:
  7.2 2.5 copy.75
  9.8 2.5 copy.79
  12.4 1.4 reshape.291
  13.8 2.5 reshape_reshape.6
  16.4 10.3 %copy.70 = bf16[2,768,2304]{1,2,0:T(8,128)(2,1)} copy(bf16[2,768,2304]{2,1,0:T(8,128)(2,1)} %param.25) | data formatting | bytes 14155776 | tf_op args[5]
  26.7 10.4 %copy.65 = bf16[2,768,2304]{1,2,0:T(8,128)(2,1)} copy(bf16[2,768,2304]{2,1,0:T(8,128)(2,1)} %param.24) | data formatting | bytes 14155776 | tf_op args[4]
  37.1 0.5 reshape.292
  37.6 0.2 fusion.59
  38.6 1.4 reshape.294
  40.0 1.4 fusion.107
  41.4 4.9 %bitcast_reduce_fusion = (f32[2,32,36]{1,2,0:T(8,128)S(1)}, f32[2,36,768,32]{2,3,1,0:T(8,128)S(1)}) fusion(pred[2,768]{1,0:T(4,128)(4,1)S(1)} %iota_compare_fusion.4, bf16[2,768,36,64]{1,3,2,0:T(8,128)(2,1)} %bitcast.124, bf16[2,32,36,64]{3,2,1,0:T(8,128)(2,1)} %copy-done.10), kind=kOutput, calls=%fused_computation.11 | convolution fusion | flops 231798528 | bytes 14461440 | tf_op jit(solution)/shard_map/bthd,bchd->bthc/dot_general | solution.py:63
  46.4 3.3 %fusion.24 = f32[2,36,32,64]{3,2,1,0:T(8,128)} fusion(bf16[2,768,36,64]{1,3,2,0:T(8,128)(2,1)S(1)} %bitcast.128, f32[2,36,768,32]{2,3,1,0:T(8,128)S(1)} %get-tuple-element.15, f32[2,32,36]{1,2,0:T(8,128)S(1)} %max.36, pred[2,768]{1,0:T(4,128)(4,1)S(1)} %iota_compare_fusion.4), kind=kOutput, calls=%fused_computation.31 | convolution fusion | flops 233570304 | bytes 14756352 | tf_op jit(solution)/shard_map/bthc,bchd->bthd/dot_general | solution.py:79
  49.7 2.4 fusion.37
  52.5 0.3 fusion.63
  52.9 4.0 %fusion.10 = f32[2,32,36]{1,2,0:T(8,128)S(1)} fusion(f32[2,36,768,32]{2,3,1,0:T(8,128)} %copy-done.2, f32[2,32,36]{1,2,0:T(8,128)S(1)} %max.36, pred[2,768]{1,0:T(4,128)(4,1)S(1)} %iota_compare_fusion.4), kind=kLoop, calls=%fused_computation.20 | loop fusion | flops 7075584 | bytes 7097856 | tf_op jit(solution)/shard_map/reduce_sum | solution.py:78
  58.0 12.5 %copy.76 = bf16[2,512,2304]{1,2,0:T(8,128)(2,1)} copy(bf16[2,512,2304]{2,0,1:T(2,128)(2,1)} %all-gather.4.cloned.1.call-done) | data formatting | bytes 9437184 | tf_op jit(solution)/shard_map/all_gather | solution.py:99
  70.5 3.4 %fusion.2 = (f32[64,36]{0,1:T(8,128)S(1)}, f32[36,2,512,64]{2,3,1,0:T(8,128)S(1)}) fusion(pred[64,2]{0,1:T(4,128)(4,1)S(1)} %iota_compare_fusion.5, bf16[2,512,36,64]{1,3,2,0:T(8,128)(2,1)} %bitcast.125, bf16[64,36,64,1]{2,1,0,3:T(8,128)(2,1)S(1)} %bitcast.130), kind=kOutput, calls=%fused_computation.9 | convolution fusion | flops 309065472 | bytes 14460032 | tf_op jit(solution)/shard_map/rhd,gkhd->rhgk/dot_general | solution.py:105
  73.9 2.3 fusion
  76.2 1.6 copy-done.1
  77.8 0.4 bitcast_multiply_fusion
  78.1 14.3 %all-gather.6.cloned.1.call-done = bf16[2,512,2304]{2,0,1:T(2,128)(2,1)} async-done(((bf16[2,64,2304]{2,0,1:T(2,128)(2,1)}), bf16[2,512,2304]{2,0,1:T(2,128)(2,1)}) %all-gather.6.cloned.1.call-update) | async-done | bytes 4718608 | tf_op jit(solution)/shard_map/all_gather | solution.py:100
  92.4 12.4 %copy.80 = bf16[2,512,2304]{1,2,0:T(8,128)(2,1)} copy(bf16[2,512,2304]{2,0,1:T(2,128)(2,1)} %all-gather.6.cloned.1.call-done) | data formatting | bytes 9437184 | tf_op jit(solution)/shard_map/all_gather | solution.py:100
  104.8 7.3 %divide_convert_fusion = bf16[64,36,64]{2,0,1:T(8,128)(2,1)S(1)} fusion(f32[64,36,64]{2,0,1:T(8,128)S(1)} %bitcast_multiply_fusion, bf16[2,512,36,64]{1,3,2,0:T(8,128)(2,1)} %bitcast.129, f32[36,2,512,64]{2,3,1,0:T(8,128)} %copy-done.1, f32[64,36]{0,1:T(8,128)S(1)} %max.38, pred[64,2]{0,1:T(4,128)(4,1)S(1)} %iota_compare_fusion.5, ...), kind=kOutput, calls=%fused_computation.46 | convolution fusion | flops 311869440 | bytes 15059072 | tf_op jit(solution)/shard_map/rhgk,gkhd->rhd/dot_general | solution.py:113
  112.1 0.4 copy.83
  112.5 0.4 convert_element_type.75
  112.9 0.2 multiply_reduce_fusion.1
  113.4 0.3 broadcast_in_dim.88
  113.7 0.2 reshape.339
  113.9 1.6 scatter_custom_fusion
  115.5 0.2 reshape_reshape.7
  115.7 16.2 %all_to_all.10 = bf16[8,18,2304]{2,1,0:T(8,128)(2,1)S(1)} all-to-all(bf16[8,18,2304]{2,1,0:T(8,128)(2,1)S(1)} %reshape_reshape.7), channel_id=1, replica_groups=mesh['req'=4,'exp'=8] {'exp'}, dimensions={0} | all-to-all | bytes 1327104 | tf_op jit(solution)/shard_map/all_to_all | solution.py:149
  131.9 1.0 reshape.301
  133.0 54.6 %all-gather.8.cloned.1.call-done = bf16[576,2304]{1,0:T(8,128)(2,1)} async-done(((bf16[144,2304]{1,0:T(8,128)(2,1)}), bf16[576,2304]{1,0:T(8,128)(2,1)}) %all-gather.8.cloned.1.call-update) | async-done | bytes 2654224 | tf_op jit(solution)/shard_map/all_gather | solution.py:150
  187.6 9.7 %fusion.8 = f32[576,1440]{1,0:T(8,128)} fusion(bf16[576,2304]{1,0:T(8,128)(2,1)} %all-gather.8.cloned.1.call-done, bf16[1,2304,1440]{1,2,0:T(8,128)(2,1)} %param.33), kind=kOutput, calls=%fused_computation.18 | convolution fusion | flops 3822059520 | bytes 12607488 | tf_op jit(solution)/shard_map/dot_general | solution.py:151
  197.3 16.7 %fusion.21 = bf16[576,2304]{1,0:T(8,128)(2,1)} fusion(bf16[1,1440,2304]{2,1,0:T(8,128)(2,1)} %param.35, f32[576,1440]{1,0:T(8,128)} %fusion.8, bf16[576,2304]{1,0:T(8,128)(2,1)} %all-gather.8.cloned.1.call-done, bf16[1,2304,1440]{1,2,0:T(8,128)(2,1)} %param.34), kind=kOutput, calls=%fused_computation.30 | convolution fusion | flops 7650422784 | bytes 21897216 | tf_op jit(solution)/shard_map/dot_general | solution.py:155
  214.4 0.8 gather_fusion.2
  215.3 0.8 gather_fusion.3
  216.8 0.7 pad_maximum_fusion
  217.4 48.2 %reduce-scatter.2.cloned.1.call-done = bf16[144,2304]{1,0:T(8,128)(2,1)} async-done(((bf16[576,2304]{1,0:T(8,128)(2,1)}), bf16[144,2304]{1,0:T(8,128)(2,1)}) %reduce-scatter.2.cloned.1.call-update) | async-done | bytes 663568 | tf_op jit(solution)/shard_map/reduce_scatter | solution.py:154
  265.6 2.2 reshape.302
  267.8 3.8 %all-to-all-start.1 = ((bf16[8,18,2304]{2,1,0:T(8,128)(2,1)}), bf16[8,18,2304]{2,1,0:T(8,128)(2,1)S(1)}, u32[]{:S(2)}, u32[]{:S(2)}) async-start(bf16[8,18,2304]{2,1,0:T(8,128)(2,1)} %reshape.302), calls=%async_computation.2 | async-start | bytes 1769472 | tf_op jit(solution)/shard_map/all_to_all | solution.py:160
  271.7 1.1 gather_fusion.1
  273.2 11.9 %all-to-all-done.1 = bf16[8,18,2304]{2,1,0:T(8,128)(2,1)S(1)} async-done(((bf16[8,18,2304]{2,1,0:T(8,128)(2,1)}), bf16[8,18,2304]{2,1,0:T(8,128)(2,1)S(1)}, u32[]{:S(2)}, u32[]{:S(2)}) %all-to-all-start.1) | async-done | bytes 663584 | tf_op jit(solution)/shard_map/all_to_all | solution.py:160
  285.1 0.2 reshape.308
  285.3 1.1 gather_fusion
  286.4 0.7 reshape.322
  287.1 1.6 multiply_reduce_fusion
  288.8 0.8 add_convert_fusion
  (108 shorter events, 4.3 us)
Async XLA Ops:
  7.2 264.4 %copy-start = (bf16[2304,8]{0,1:T(8,128)(2,1)S(1)}, bf16[2304,8]{0,1:T(8,128)(2,1)}, u32[]{:S(2)}) copy-start(bf16[2304,8]{0,1:T(8,128)(2,1)} %param.32) | copy-start | bytes 110596
  7.2 50.8 %all-gather.4.cloned.1.call-start = ((), (), s32[]{:S(2)}) async-start(), calls=%async_computation.3 | async-start | bytes 5308416 | tf_op jit(solution)/shard_map/all_gather | solution.py:99
  9.8 82.6 %all-gather.6.cloned.1.call-start = ((), (), s32[]{:S(2)}) async-start(), calls=%async_computation.4 | async-start | bytes 5308416 | tf_op jit(solution)/shard_map/all_gather | solution.py:100
  12.3 175.2 %all-gather.8.cloned.1.call-start = ((), (), s32[]{:S(2)}) async-start(), calls=%async_computation.5 | async-start | bytes 3317760 | tf_op jit(solution)/shard_map/all_gather | solution.py:150
  13.8 26.2 %copy-start.10 = (bf16[2,32,36,64]{3,2,1,0:T(8,128)(2,1)}, bf16[2,32,36,64]{3,2,1,0:T(8,128)(2,1)S(1)}, u32[]{:S(2)}) copy-start(bf16[2,32,36,64]{3,2,1,0:T(8,128)(2,1)S(1)} %reshape.291) | copy-start | bytes 884740
  26.7 10.4 %copy-start.4 = (bf16[2,32,2304]{2,1,0:T(8,128)(2,1)S(1)}, bf16[2,32,2304]{2,1,0:T(8,128)(2,1)}, u32[]{:S(2)}) copy-start(bf16[2,32,2304]{2,1,0:T(8,128)(2,1)} %param.21) | copy-start | bytes 884740
  26.7 10.9 %copy-start.17 = (s32[2,32]{1,0:T(2,128)S(1)}, s32[2,32]{1,0:T(2,128)}, u32[]{:S(2)}) copy-start(s32[2,32]{1,0:T(2,128)} %param.23) | copy-start | bytes 772
  26.7 11.9 %copy-start.5 = (bf16[2,32,2304]{2,1,0:T(8,128)(2,1)S(1)}, bf16[2,32,2304]{2,1,0:T(8,128)(2,1)}, u32[]{:S(2)}) copy-start(bf16[2,32,2304]{2,1,0:T(8,128)(2,1)} %param.22) | copy-start | bytes 884740
  26.7 13.2 %copy-start.16 = (s32[2]{0:T(128)S(1)}, s32[2]{0:T(128)}, u32[]{:S(2)}) copy-start(s32[2]{0:T(128)} %param.26) | copy-start | bytes 28
  40.0 6.4 %slice-start = ((s8[7077888]{0:T(1024)(128)(4,1)}), s8[4194304]{0:T(1024)(128)(4,1)S(1)}, s32[]{:S(2)}) async-start(s8[7077888]{0:T(1024)(128)(4,1)} %bitcast.126), calls=%async_computation.7 | async-start | bytes 8388608
  41.4 5.0 %slice-start.1 = ((s8[7077888]{0:T(1024)(128)(4,1)}), s8[2883584]{0:T(1024)(128)(4,1)S(1)}, s32[]{:S(2)}) async-start(s8[7077888]{0:T(1024)(128)(4,1)} %bitcast.126), calls=%async_computation.8 | async-start | bytes 5767168
  46.3 3.4 %copy-start.2 = (f32[2,36,768,32]{2,3,1,0:T(8,128)}, f32[2,36,768,32]{2,3,1,0:T(8,128)S(1)}, u32[]{:S(2)}) copy-start(f32[2,36,768,32]{2,3,1,0:T(8,128)S(1)} %get-tuple-element.15) | copy-start | bytes 21233668
  49.7 2.6 copy-start.18
  49.7 2.8 copy-start.3
  52.3 4.7 %copy-start.13 = (s32[2,32,2]{1,2,0:T(2,128)S(1)}, s32[2,32,2]{1,2,0:T(2,128)}, u32[]{:S(2)}) copy-start(s32[2,32,2]{1,2,0:T(2,128)} %param.36) | copy-start | bytes 1540
  57.9 12.5 %copy-start.9 = (bf16[64,36,64]{2,1,0:T(8,128)(2,1)S(1)}, bf16[64,36,64]{2,1,0:T(8,128)(2,1)}, u32[]{:S(2)}) copy-start(bf16[64,36,64]{2,1,0:T(8,128)(2,1)} %reshape_reshape.6) | copy-start | bytes 884740
  73.8 3.9 %copy-start.1 = (f32[36,2,512,64]{2,3,1,0:T(8,128)}, f32[36,2,512,64]{2,3,1,0:T(8,128)S(1)}, u32[]{:S(2)}) copy-start(f32[36,2,512,64]{2,3,1,0:T(8,128)S(1)} %get-tuple-element.19) | copy-start | bytes 28311556
  104.8 8.1 %copy-start.11 = (bf16[2,32,2304]{2,1,0:T(8,128)(2,1)S(1)}, bf16[2,32,2304]{2,1,0:T(8,128)(2,1)}, u32[]{:S(2)}) copy-start(bf16[2,32,2304]{2,1,0:T(8,128)(2,1)} %param.30) | copy-start | bytes 884740
  104.8 8.5 %copy-start.14 = (f32[2304]{0:T(1024)S(1)}, f32[2304]{0:T(1024)}, u32[]{:S(2)}) copy-start(f32[2304]{0:T(1024)} %param.31) | copy-start | bytes 27652
  112.9 1.0 copy-start.7
  133.0 132.6 %reduce-scatter.2.cloned.1.call-start = ((), (), s32[]{:S(2)}) async-start(), calls=%async_computation.6 | async-start | bytes 3317760 | tf_op jit(solution)/shard_map/reduce_scatter | solution.py:154
  197.3 17.0 %copy-start.15 = (s32[2,8]{1,0:T(2,128)S(1)}, s32[2,8]{1,0:T(2,128)}, u32[]{:S(2)}) copy-start(s32[2,8]{1,0:T(2,128)} %param.37) | copy-start | bytes 196
  197.3 17.9 %copy-start.6 = (bf16[2,32,2304]{2,1,0:T(8,128)(2,1)S(1)}, bf16[2,32,2304]{2,1,0:T(8,128)(2,1)}, u32[]{:S(2)}) copy-start(bf16[2,32,2304]{2,1,0:T(8,128)(2,1)} %param.22) | copy-start | bytes 884740
  267.8 17.3 %all-to-all-start.1 = ((bf16[8,18,2304]{2,1,0:T(8,128)(2,1)}), bf16[8,18,2304]{2,1,0:T(8,128)(2,1)S(1)}, u32[]{:S(2)}, u32[]{:S(2)}) async-start(bf16[8,18,2304]{2,1,0:T(8,128)(2,1)} %reshape.302), calls=%async_computation.2 | async-start | bytes 1769472 | tf_op jit(solution)/shard_map/all_to_all | solution.py:160
  285.3 3.5 %copy-start.8 = (bf16[2,32,2304]{2,1,0:T(8,128)(2,1)S(1)}, bf16[2,32,2304]{2,1,0:T(8,128)(2,1)}, u32[]{:S(2)}) copy-start(bf16[2,32,2304]{2,1,0:T(8,128)(2,1)} %copy-done.7) | copy-start | bytes 884740
  285.3 3.5 %copy-start.12 = (bf16[2,32,2304]{2,1,0:T(8,128)(2,1)S(1)}, bf16[2,32,2304]{2,1,0:T(8,128)(2,1)}, u32[]{:S(2)}) copy-start(bf16[2,32,2304]{2,1,0:T(8,128)(2,1)} %param.30) | copy-start | bytes 884740
Sparse Core Ops, SparseCore 0:
  9.9 41.6 all-gather.3
  53.4 38.9 all-gather.5
  133.1 54.4 all-gather.7
  214.2 51.3 reduce-scatter.1
where the time goes:
time: 298 us; the launch traced here: 296 us
  waiting for transfers between devices  129 us (43%)
  local copies, waits for them, and re-layouts  71.3 us (24%)
  matrix products  50.2 us (17%)
  blocking collectives  16.2 us (5%)
  between operations  14.3 us (5%)
  other arithmetic  11.3 us (4%)
  starting transfers between devices  3.93 us (1%)
    all_gather x1, waiting for transfers between devices, on_device(): lax.all_gather(arrived.reshape(-1, width), 'req', axis=0, tiled=True)  54.6 us
    reduce_scatter x1, waiting for transfers between devices, on_device(): lax.psum_scatter(jnp.dot(hidden, down_local, preferred_element_type=jnp.f...  48.2 us
    unnamed x48, local copies, waits for them, and re-layouts  27.5 us
    dot_general x1, matrix products, on_device(): jnp.dot(hidden, down_local, preferred_element_type=jnp.float32)  16.7 us
    all_to_all x1, blocking collectives, on_device(): lax.all_to_all(outgoing, 'exp', split_axis=0, concat_axis=0, tiled=True)  16.2 us
    all_gather x1, waiting for transfers between devices, on_device(): value_piece = lax.all_gather(prompt_values, 'exp', axis=1, tiled=True)  14.3 us
    all_gather x1, local copies, waits for them, and re-layouts, on_device(): key_piece = lax.all_gather(prompt_keys, 'exp', axis=1, tiled=True)  12.5 us
    all_gather x1, local copies, waits for them, and re-layouts, on_device(): value_piece = lax.all_gather(prompt_values, 'exp', axis=1, tiled=True)  12.4 us
  transfers between devices with their start and end apart: 5, of which 4 were waited for; matrix products, arithmetic and copies ran while one was open for 24% of the time, Pallas kernels for 0%

commit v1 on v0

--- a/solution.py
+++ b/solution.py
@@ -96,8 +96,13 @@
     running_top = local_top
     summed = local_total
     gathered_acc = local_acc
-    key_piece = lax.all_gather(prompt_keys, "exp", axis=1, tiled=True)
-    value_piece = lax.all_gather(prompt_values, "exp", axis=1, tiled=True)
+    key_piece, value_piece = jnp.split(
+        jax.lax.all_gather(
+            jnp.concatenate([prompt_keys, prompt_values], 0), "exp", axis=1, tiled=True
+        ),
+        [prompt_keys.shape[0]],
+        0,
+    )
     key_count = key_piece.shape[1]
     key_heads = key_piece.reshape(GRP, key_count, HEADS, HDIM)
     value_heads = value_piece.reshape(GRP, key_count, HEADS, HDIM)

time: 298 us -> 306 us (1.027)
  local copies, waits for them, and re-layouts: 71.3 us -> 83.6 us
  matrix products: 50.2 us -> 45.6 us
    all_gather x2 -> x0, local copies, waits for them, and re-layouts: 24.9 us -> none  [the longest x1 12.5 us: on_device(): key_piece = lax.all_gather(prompt_keys, 'exp', axis=1, tiled=True)]
    unnamed x48 -> x40, local copies, waits for them, and re-layouts: 27.5 us -> 51.7 us
    split x0 -> x1, local copies, waits for them, and re-layouts: none -> 12.4 us  [on_device(): jnp.split(jax.lax.all_gather(jnp.concatenate([prompt_keys, prompt_values]...]
    dot_general x1, matrix products: 7.34 us -> 1.38 us  [on_device(): jnp.einsum('rhgk,gkhd->rhd', block_weights.astype(jnp.bfloat16), value_he...]
    dot_general x1, matrix products: 3.3 us -> 7.17 us  [on_device(): jnp.einsum('bthc,bchd->bthd', cache_weights.astype(jnp.bfloat16), cache_v...]
    all_gather x2 -> x1, waiting for transfers between devices: 14.3 us -> 14.9 us  [on_device(): jax.lax.all_gather(jnp.concatenate([prompt_keys, prompt_values], 0), 'exp...]
  transfers between devices with their start and end apart: 5 -> 4, of which waited for: 4 -> 4; matrix products, arithmetic and copies ran while one was open for 24% -> 16% of each run, Pallas kernels for 0% -> 0%
where the time goes in v1:
time: 306 us; the launch traced here: 304 us
  waiting for transfers between devices  130 us (42%)
  local copies, waits for them, and re-layouts  83.6 us (27%)
  matrix products  45.6 us (15%)
  blocking collectives  16.1 us (5%)
  between operations  14.3 us (5%)
  other arithmetic  11.3 us (4%)
  starting transfers between devices  3.93 us (1%)
    all_gather x1, waiting for transfers between devices, on_device(): lax.all_gather(arrived.reshape(-1, width), 'req', axis=0, tiled=True)  54.6 us
    unnamed x40, local copies, waits for them, and re-layouts  51.7 us
    reduce_scatter x1, waiting for transfers between devices, on_device(): lax.psum_scatter(jnp.dot(hidden, down_local, preferred_element_type=jnp.f...  48.2 us
    dot_general x1, matrix products, on_device(): jnp.dot(hidden, down_local, preferred_element_type=jnp.float32)  16.7 us
    all_to_all x1, blocking collectives, on_device(): lax.all_to_all(outgoing, 'exp', split_axis=0, concat_axis=0, tiled=True)  16.1 us
    all_gather x1, waiting for transfers between devices, on_device(): jax.lax.all_gather(jnp.concatenate([prompt_keys, prompt_values], 0), 'exp...  14.9 us
    split x1, local copies, waits for them, and re-layouts, on_device(): jnp.split(jax.lax.all_gather(jnp.concatenate([prompt_keys, prompt_values]...  12.4 us
    all_to_all x1, waiting for transfers between devices, on_device(): lax.all_to_all(summed_rows.reshape(holder_count, CAP, width), 'exp', spli...  11.9 us
  transfers between devices with their start and end apart: 4, of which 4 were waited for; matrix products, arithmetic and copies ran while one was open for 16% of the time, Pallas kernels for 0%

profile of v1, /device:TPU:0, one launch (start us, length us, event | category | flops | bytes accessed | tf_op | source)
XLA Modules:
  0.0 304.4 jit_solution(5355220500571321052)
XLA Ops:
  7.2 1.7 copy.78
  8.9 1.7 copy.79
  10.6 2.2 pad_maximum_fusion
  12.9 0.5 reshape.291
  13.4 0.5 reshape_reshape.6
  13.9 10.5 %copy.68 = bf16[2,768,2304]{1,2,0:T(8,128)(2,1)} copy(bf16[2,768,2304]{2,1,0:T(8,128)(2,1)} %param.24) | data formatting | bytes 14155776 | tf_op args[4]
  24.4 1.3 reshape.292
  25.7 0.2 fusion.50
  26.8 1.5 fusion.95
  28.3 4.4 %bitcast_reduce_fusion = (f32[2,32,36]{1,2,0:T(8,128)S(1)}, f32[2,36,768,32]{2,3,1,0:T(8,128)S(1)}) fusion(pred[2,768]{1,0:T(4,128)(4,1)S(1)} %iota_compare_fusion.4, bf16[2,768,36,64]{1,3,2,0:T(8,128)(2,1)} %bitcast.116, bf16[2,32,36,64]{3,2,1,0:T(8,128)(2,1)S(1)} %reshape.291), kind=kOutput, calls=%fused_computation.11 | convolution fusion | flops 231798528 | bytes 14461440 | tf_op jit(solution)/shard_map/bthd,bchd->bthc/dot_general | solution.py:63
  32.8 0.3 fusion.54
  33.1 2.5 copy-done.1
  35.6 1.7 fusion.10
  37.7 10.4 %copy.73 = bf16[2,768,2304]{1,2,0:T(8,128)(2,1)} copy(bf16[2,768,2304]{2,1,0:T(8,128)(2,1)} %param.25) | data formatting | bytes 14155776 | tf_op args[5]
  48.2 1.3 reshape.294
  49.5 7.2 %fusion.19 = f32[2,36,32,64]{3,2,1,0:T(8,128)S(1)} fusion(bf16[2,768,36,64]{1,3,2,0:T(8,128)(2,1)} %bitcast.118, f32[2,36,768,32]{2,3,1,0:T(8,128)} %copy-done.1, f32[2,32,36]{1,2,0:T(8,128)S(1)} %max.36, pred[2,768]{1,0:T(4,128)(4,1)S(1)} %iota_compare_fusion.4), kind=kOutput, calls=%fused_computation.27 | convolution fusion | flops 233570304 | bytes 14756352 | tf_op jit(solution)/shard_map/bthc,bchd->bthd/dot_general | solution.py:79
  56.7 0.4 fusion.30
  57.3 1.4 copy.83
  59.6 14.9 %all-gather.3.cloned.1.call-done = bf16[4,512,2304]{2,0,1:T(4,128)(2,1)} async-done(((bf16[4,64,2304]{2,0,1:T(4,128)(2,1)}), bf16[4,512,2304]{2,0,1:T(4,128)(2,1)}) %all-gather.3.cloned.1.call-update) | async-done | bytes 9437200 | tf_op jit(solution)/shard_map/all_gather | solution.py:100
  74.5 12.4 %fusion.94 = (bf16[2,512,2304]{2,0,1:T(2,128)(2,1)}, bf16[2,512,2304]{2,0,1:T(2,128)(2,1)}) fusion(bf16[4,512,2304]{2,0,1:T(4,128)(2,1)} %all-gather.3.cloned.1.call-done), kind=kLoop, calls=%fused_computation.134 | loop fusion | bytes 18874368 | tf_op jit(solution)/shard_map/split | solution.py:99
  86.9 12.3 %copy.101 = bf16[2,512,2304]{1,2,0:T(8,128)(2,1)} copy(bf16[2,512,2304]{2,0,1:T(2,128)(2,1)} %get-tuple-element.13) | data formatting | bytes 9437184
  99.2 12.4 %copy.102 = bf16[2,512,2304]{1,2,0:T(8,128)(2,1)} copy(bf16[2,512,2304]{2,0,1:T(2,128)(2,1)} %get-tuple-element.14) | data formatting | bytes 9437184
  111.6 3.4 %fusion.2 = (f32[64,36]{0,1:T(8,128)S(1)}, f32[36,2,512,64]{2,3,1,0:T(8,128)S(1)}) fusion(pred[64,2]{0,1:T(4,128)(4,1)S(1)} %iota_compare_fusion.5, bf16[2,512,36,64]{1,3,2,0:T(8,128)(2,1)} %bitcast.117, bf16[64,36,64,1]{2,1,0,3:T(8,128)(2,1)S(1)} %bitcast.121), kind=kOutput, calls=%fused_computation.9 | convolution fusion | flops 309065472 | bytes 14460032 | tf_op jit(solution)/shard_map/rhd,gkhd->rhgk/dot_general | solution.py:110
  115.0 2.7 fusion
  117.8 1.4 divide_convert_fusion
  119.2 0.4 copy.87
  119.6 0.4 convert_element_type.75
  120.0 0.2 multiply_reduce_fusion.1
  120.4 0.3 broadcast_in_dim.88
  120.7 1.0 reshape.339
  121.8 2.1 scatter_custom_fusion
  124.1 16.1 %all_to_all.10 = bf16[8,18,2304]{2,1,0:T(8,128)(2,1)S(1)} all-to-all(bf16[8,18,2304]{2,1,0:T(8,128)(2,1)S(1)} %reshape_reshape.7), channel_id=1, replica_groups=mesh['req'=4,'exp'=8] {'exp'}, dimensions={0} | all-to-all | bytes 1327104 | tf_op jit(solution)/shard_map/all_to_all | solution.py:154
  140.3 1.0 reshape.301
  141.4 54.6 %all-gather.5.cloned.1.call-done = bf16[576,2304]{1,0:T(8,128)(2,1)} async-done(((bf16[144,2304]{1,0:T(8,128)(2,1)}), bf16[576,2304]{1,0:T(8,128)(2,1)}) %all-gather.5.cloned.1.call-update) | async-done | bytes 2654224 | tf_op jit(solution)/shard_map/all_gather | solution.py:155
  195.9 9.7 %fusion.8 = f32[576,1440]{1,0:T(8,128)} fusion(bf16[576,2304]{1,0:T(8,128)(2,1)} %all-gather.5.cloned.1.call-done, bf16[1,2304,1440]{1,2,0:T(8,128)(2,1)} %param.33), kind=kOutput, calls=%fused_computation.18 | convolution fusion | flops 3822059520 | bytes 12607488 | tf_op jit(solution)/shard_map/dot_general | solution.py:156
  205.7 16.7 %fusion.16 = bf16[576,2304]{1,0:T(8,128)(2,1)} fusion(bf16[1,1440,2304]{2,1,0:T(8,128)(2,1)} %param.35, f32[576,1440]{1,0:T(8,128)} %fusion.8, bf16[576,2304]{1,0:T(8,128)(2,1)} %all-gather.5.cloned.1.call-done, bf16[1,2304,1440]{1,2,0:T(8,128)(2,1)} %param.34), kind=kOutput, calls=%fused_computation.26 | convolution fusion | flops 7650422784 | bytes 21897216 | tf_op jit(solution)/shard_map/dot_general | solution.py:160
  222.8 0.8 gather_fusion.2
  223.6 0.8 gather_fusion.3
  225.1 0.7 pad_maximum_fusion.1
  225.8 48.2 %reduce-scatter.2.cloned.1.call-done = bf16[144,2304]{1,0:T(8,128)(2,1)} async-done(((bf16[576,2304]{1,0:T(8,128)(2,1)}), bf16[144,2304]{1,0:T(8,128)(2,1)}) %reduce-scatter.2.cloned.1.call-update) | async-done | bytes 663568 | tf_op jit(solution)/shard_map/reduce_scatter | solution.py:159
  273.9 2.2 reshape.302
  276.1 3.8 %all-to-all-start.1 = ((bf16[8,18,2304]{2,1,0:T(8,128)(2,1)}), bf16[8,18,2304]{2,1,0:T(8,128)(2,1)S(1)}, u32[]{:S(2)}, u32[]{:S(2)}) async-start(bf16[8,18,2304]{2,1,0:T(8,128)(2,1)} %reshape.302), calls=%async_computation.2 | async-start | bytes 1769472 | tf_op jit(solution)/shard_map/all_to_all | solution.py:165
  280.1 1.1 gather_fusion.1
  281.6 11.9 %all-to-all-done.1 = bf16[8,18,2304]{2,1,0:T(8,128)(2,1)S(1)} async-done(((bf16[8,18,2304]{2,1,0:T(8,128)(2,1)}), bf16[8,18,2304]{2,1,0:T(8,128)(2,1)S(1)}, u32[]{:S(2)}, u32[]{:S(2)}) %all-to-all-start.1) | async-done | bytes 663584 | tf_op jit(solution)/shard_map/all_to_all | solution.py:165
  293.6 1.1 gather_fusion
  294.7 0.7 reshape.322
  295.4 1.6 multiply_reduce_fusion
  297.1 0.8 add_convert_fusion
  (96 shorter events, 4.6 us)
Async XLA Ops:
  7.2 272.8 %copy-start = (bf16[2304,8]{0,1:T(8,128)(2,1)S(1)}, bf16[2304,8]{0,1:T(8,128)(2,1)}, u32[]{:S(2)}) copy-start(bf16[2304,8]{0,1:T(8,128)(2,1)} %param.32) | copy-start | bytes 110596
  7.2 5.7 %copy-start.8 = (bf16[2,32,2304]{2,1,0:T(8,128)(2,1)S(1)}, bf16[2,32,2304]{2,1,0:T(8,128)(2,1)}, u32[]{:S(2)}) copy-start(bf16[2,32,2304]{2,1,0:T(8,128)(2,1)} %param.20) | copy-start | bytes 884740
  7.2 67.4 %all-gather.3.cloned.1.call-start = ((), (), s32[]{:S(2)}) async-start(), calls=%async_computation.3 | async-start | bytes 10616832 | tf_op jit(solution)/shard_map/all_gather | solution.py:100
  12.9 183.1 %all-gather.5.cloned.1.call-start = ((), (), s32[]{:S(2)}) async-start(), calls=%async_computation.4 | async-start | bytes 3317760 | tf_op jit(solution)/shard_map/all_gather | solution.py:155
  13.9 10.6 %copy-start.3 = (bf16[2,32,2304]{2,1,0:T(8,128)(2,1)S(1)}, bf16[2,32,2304]{2,1,0:T(8,128)(2,1)}, u32[]{:S(2)}) copy-start(bf16[2,32,2304]{2,1,0:T(8,128)(2,1)} %param.21) | copy-start | bytes 884740
  13.9 11.9 %copy-start.14 = (s32[2,32]{1,0:T(2,128)S(1)}, s32[2,32]{1,0:T(2,128)}, u32[]{:S(2)}) copy-start(s32[2,32]{1,0:T(2,128)} %param.23) | copy-start | bytes 772
  13.9 12.8 %copy-start.13 = (s32[2]{0:T(128)S(1)}, s32[2]{0:T(128)}, u32[]{:S(2)}) copy-start(s32[2]{0:T(128)} %param.26) | copy-start | bytes 28
  32.7 2.9 copy-start.1
  32.7 4.8 %copy-start.15 = (s32[2]{0:T(128)S(1)}, s32[2]{0:T(128)}, u32[]{:S(2)}) copy-start(s32[2]{0:T(128)} %param.29) | copy-start | bytes 28
  37.7 10.4 %copy-start.4 = (bf16[2,32,2304]{2,1,0:T(8,128)(2,1)S(1)}, bf16[2,32,2304]{2,1,0:T(8,128)(2,1)}, u32[]{:S(2)}) copy-start(bf16[2,32,2304]{2,1,0:T(8,128)(2,1)} %param.22) | copy-start | bytes 884740
  49.5 7.2 %copy-start.6 = (bf16[2,32,36,64]{3,2,1,0:T(8,128)(2,1)S(1)}, bf16[2,32,36,64]{3,2,1,0:T(8,128)(2,1)}, u32[]{:S(2)}) copy-start(bf16[2,32,36,64]{3,2,1,0:T(8,128)(2,1)} %reshape.294) | copy-start | bytes 884740
  56.7 2.0 copy-start.10
  115.0 2.7 copy-start.2
  115.0 2.7 copy-start.7
  117.8 2.2 copy-start.9
  117.8 2.5 copy-start.11
  120.0 177.1 %copy-start.5 = (bf16[2,32,2304]{2,1,0:T(8,128)(2,1)}, bf16[2,32,2304]{2,1,0:T(8,128)(2,1)S(1)}, u32[]{:S(2)}) copy-start(bf16[2,32,2304]{2,1,0:T(8,128)(2,1)S(1)} %convert_element_type.75) | copy-start | bytes 884740
  141.3 132.6 %reduce-scatter.2.cloned.1.call-start = ((), (), s32[]{:S(2)}) async-start(), calls=%async_computation.5 | async-start | bytes 3317760 | tf_op jit(solution)/shard_map/reduce_scatter | solution.py:159
  205.7 17.0 %copy-start.12 = (s32[2,8]{1,0:T(2,128)S(1)}, s32[2,8]{1,0:T(2,128)}, u32[]{:S(2)}) copy-start(s32[2,8]{1,0:T(2,128)} %param.37) | copy-start | bytes 196
  276.1 17.3 %all-to-all-start.1 = ((bf16[8,18,2304]{2,1,0:T(8,128)(2,1)}), bf16[8,18,2304]{2,1,0:T(8,128)(2,1)S(1)}, u32[]{:S(2)}, u32[]{:S(2)}) async-start(bf16[8,18,2304]{2,1,0:T(8,128)(2,1)} %reshape.302), calls=%async_computation.2 | async-start | bytes 1769472 | tf_op jit(solution)/shard_map/all_to_all | solution.py:165
Sparse Core Ops, SparseCore 0:
  13.0 61.5 all-gather.2
  141.5 54.4 all-gather.4
  222.5 51.3 reduce-scatter.1
